TPU v7x, 32 devices: a whole 2x2x4 slice. The times are simulated.
32 devices in a mesh: blk: 4 (over y, x), team: 4 (over z), dp: 2 (over core).
Axes of the slice: x: 2, y: 2, z: 4, core: 2. Of those that a mesh axis runs over, the one named last changes fastest.
Arguments:
- hidden: bfloat16 [1024, 28672], P(('blk', 'dp'), 'team'), may hold values from -6 to 6
- out_grad: bfloat16 [1024, 8192], P(('blk', 'dp'), 'team'), may hold values from -0.1875 to 0.1875
- act_rows: int32 [4, 64, 12], P('team'), may hold values from 0 to 55, as said below
- col_owner: int32 [64], replicated, may hold values from 0 to 3, as said below
Outputs:
- gradients: float32 [4, 4, 288, 128, 128], P('team', 'blk', 'dp')
- scores: float32 [4, 4, 288], P('team', 'blk', 'dp')
Inputs may be any that keep to these rules, and one draw needn't show every extreme that they name: For each t and c the 12 entries act_rows[t, c, :] are distinct. `col_owner`: some owner holds exactly 24 block columns and no owner holds more.
All inputs are finite; a program needn't handle non-finite values.
Results may differ from a plain program's by a relative error of at most 0.0003.
Values may be sent and summed in bfloat16 or wider, within the bound.
A program may use at most 192 MiB of HBM per device.

v0:
```python
import jax
import jax.numpy as jnp
from jax import lax
from jax.sharding import PartitionSpec as P

D = 8192
BS = 128
epsilon = 1e-06


def on_device(hidden, out_grad, act_rows, col_owner):
    owners_count = lax.axis_size("blk")
    owner_index = lax.axis_index("blk")
    column_blocks = D // BS
    capacity = min(3 * column_blocks // (2 * owners_count), 3 * column_blocks // 4)
    per_column = act_rows.shape[2]
    owners = jnp.arange(owners_count, dtype=jnp.int32)
    onehot = (col_owner[:, None] == owners[None, :]).astype(jnp.int32)
    column_rank = jnp.sum((jnp.cumsum(onehot, axis=0) - onehot) * onehot, axis=1)
    slot_ids = jnp.arange(capacity, dtype=jnp.int32)
    matches = (col_owner[None, None, :] == owners[:, None, None]) & (
        column_rank[None, None, :] == slot_ids[None, :, None]
    )
    owned_all = jnp.sum(
        matches.astype(jnp.int32) * jnp.arange(column_blocks, dtype=jnp.int32)[None, None, :],
        axis=2,
    )
    alive_all = jnp.any(matches, axis=2)
    owned_mine = lax.dynamic_index_in_dim(owned_all, owner_index, 0, keepdims=False)
    alive_mine = lax.dynamic_index_in_dim(alive_all, owner_index, 0, keepdims=False)
    block_rows = jnp.take(act_rows[0], owned_mine, axis=0).reshape(-1)
    grad_full = lax.all_gather(out_grad, "team", axis=1, tiled=True)
    grad_mask = alive_mine.astype(jnp.bfloat16)[None, :, None]
    hidden_piece = lax.all_gather(hidden, "blk", axis=0, tiled=True)
    grad_piece = lax.all_gather(grad_full, "blk", axis=0, tiled=True)
    count_rows = grad_piece.shape[0]
    picked_grad = (
        jnp.take(grad_piece.reshape(count_rows, column_blocks, BS), owned_mine, axis=1) * grad_mask
    )
    count_rows = hidden_piece.shape[0]
    hidden_blocks = hidden_piece.reshape(count_rows, -1, BS)
    picked_hidden = jnp.take(hidden_blocks, block_rows, axis=1).reshape(
        count_rows, capacity, per_column, BS
    )
    partial_value = jnp.einsum(
        "ncki,ncj->ckij", picked_hidden, picked_grad, preferred_element_type=jnp.float32
    )
    partial_value = partial_value.reshape(capacity * per_column, BS, BS)
    gradients = lax.psum_scatter(partial_value, "dp", scatter_dimension=0, tiled=True)
    scores = jnp.sqrt(jnp.mean(gradients * gradients, axis=(1, 2)) + epsilon)
    return (gradients[None, None], scores[None, None])


def solution(mesh):
    in_specs = (P(("blk", "dp"), "team"), P(("blk", "dp"), "team"), P("team", None, None), P())
    out_specs = (P("team", "blk", "dp", None, None), P("team", "blk", "dp"))
    return jax.shard_map(
        on_device, mesh=mesh, in_specs=in_specs, out_specs=out_specs, check_vma=False
    )
```

profile of v0, /device:TPU:0, one launch (start us, length us, event | category | flops | bytes accessed | tf_op | source)
XLA Modules:
  0.0 305.4 jit_solution(6852745690831261006)
XLA Ops:
  7.2 2.0 copy.20
  9.3 0.0 all-gather.4.cloned.1.call-start
  9.3 3.9 %copy.17 = bf16[128,7168]{0,1:T(8,128)(2,1)} copy(bf16[128,7168]{1,0:T(8,128)(2,1)} %param.4) | data formatting | bytes 3670016 | tf_op args[0]
  13.3 44.7 %all-gather.6.cloned.1.call-done = bf16[128,8192]{0,1:T(8,128)(2,1)} async-done(((bf16[128,2048]{0,1:T(8,128)(2,1)}), bf16[128,8192]{0,1:T(8,128)(2,1)}) %all-gather.6.cloned.1.call-update) | async-done | bytes 2097168 | tf_op jit(solution)/shard_map/all_gather | solution.py:32
  58.1 0.1 fusion.11
  58.1 0.1 reduce_window_sum.11
  58.2 0.1 copy.16
  58.3 0.2 select_reduce_fusion
  58.5 0.1 fusion.10
  58.7 0.6 gather_fusion
  59.3 0.1 compare_and_fusion
  59.4 0.1 select_n.73
  59.5 0.2 and_reduce_fusion
  59.7 78.1 %all-gather.4.cloned.1.call-done = bf16[512,7168]{0,1:T(8,128)(2,1)} async-done(((bf16[128,7168]{0,1:T(8,128)(2,1)}), bf16[512,7168]{0,1:T(8,128)(2,1)}) %all-gather.4.cloned.1.call-update) | async-done | bytes 7340048 | tf_op jit(solution)/shard_map/all_gather | solution.py:34
  137.8 10.4 %copy.18 = bf16[512,56,128]{2,0,1:T(8,128)(2,1)} copy(bf16[512,56,128]{0,2,1:T(8,128)(2,1)} %bitcast.28) | data formatting | bytes 14680064 | tf_op jit(solution)/shard_map/reshape | solution.py:41
  148.3 18.8 %gather_fusion.1 = bf16[288,512,128]{2,1,0:T(8,128)(2,1)} fusion(bf16[512,56,128]{2,0,1:T(8,128)(2,1)} %copy.18, s32[1024]{0:T(1024)S(1)} %pad_clamp_fusion), kind=kCustom, calls=%fused_computation.1 | custom fusion | bytes 75498624 | tf_op jit(solution)/shard_map/jit(_take)/gather | solution.py:42
  167.1 48.8 %copy.19 = bf16[512,24,12,128]{0,3,2,1:T(8,128)(2,1)} copy(bf16[512,24,12,128]{3,0,2,1:T(8,128)(2,1)} %bitcast.24) | data formatting | bytes 75497472 | tf_op jit(solution)/shard_map/jit(_take)/gather | solution.py:42
  215.8 11.2 %all-gather.8.cloned.1.call-done = bf16[512,8192]{0,1:T(8,128)(2,1)} async-done(((bf16[128,8192]{0,1:T(8,128)(2,1)}), bf16[512,8192]{0,1:T(8,128)(2,1)}) %all-gather.8.cloned.1.call-update) | async-done | bytes 8388624 | tf_op jit(solution)/shard_map/all_gather | solution.py:35
  227.0 11.9 %copy.21 = bf16[512,64,128]{2,0,1:T(8,128)(2,1)} copy(bf16[512,64,128]{0,2,1:T(8,128)(2,1)} %bitcast.27) | data formatting | bytes 16777216 | tf_op jit(solution)/shard_map/reshape | solution.py:38
  238.9 4.5 %gather_fusion.2 = bf16[24,512,128]{2,1,0:T(8,128)(2,1)S(1)} fusion(bf16[512,64,128]{2,0,1:T(8,128)(2,1)} %copy.21, s32[1024]{0:T(1024)S(1)} %pad_clamp_fusion.1), kind=kCustom, calls=%fused_computation.2 | custom fusion | bytes 6291552 | tf_op jit(solution)/shard_map/jit(_take)/gather | solution.py:38
  243.5 23.4 %fusion = f32[24,12,128,128]{3,2,1,0:T(8,128)} fusion(bf16[512,24,12,128]{0,3,2,1:T(8,128)(2,1)} %copy.19, pred[24,12]{1,0:T(8,128)(4,1)S(1)} %get-tuple-element.2, bf16[24,512,128]{2,1,0:T(8,128)(2,1)S(1)} %gather_fusion.2, pred[24]{0:T(512)(128)(4,1)S(1)} %compare_and_fusion.1, bf16[24]{0:T(256)(128)(2,1)S(1)} %fusion.13), kind=kOutput, calls=%fused_computation.3 | convolution fusion | flops 4853858304 | bytes 59769192 | tf_op jit(solution)/shard_map/ncki,ncj->ckij/dot_general | solution.py:45
  266.9 26.7 %reduce-scatter.2.cloned.1.call-done = f32[144,128,128]{2,1,0:T(8,128)} async-done(((f32[288,128,128]{2,1,0:T(8,128)}), f32[144,128,128]{2,1,0:T(8,128)}) %reduce-scatter.2.cloned.1.call-update) | async-done | bytes 9437200 | tf_op jit(solution)/shard_map/reduce_scatter | solution.py:49
  293.6 4.7 %multiply_reduce_fusion = f32[144]{0:T(256)S(1)} fusion(f32[144,128,128]{2,1,0:T(8,128)} %reduce-scatter.2.cloned.1.call-done), kind=kLoop, calls=%fused_computation.7 | loop fusion | flops 4718448 | bytes 9437760 | tf_op jit(solution)/shard_map/reduce_sum | solution.py:50
  298.3 0.6 add_sqrt_fusion
  (19 shorter events, 0.3 us)
Async XLA Ops:
  7.2 50.9 %copy-start.1 = (s32[64]{0:T(128)S(1)}, s32[64]{0:T(128)}, u32[]{:S(2)}) copy-start(s32[64]{0:T(128)} %param.7) | copy-start | bytes 772
  7.2 51.1 %copy-start = (s32[1,64,12]{1,0,2:T(1,128)S(1)}, s32[1,64,12]{1,0,2:T(1,128)}, u32[]{:S(2)}) copy-start(s32[1,64,12]{1,0,2:T(1,128)} %param.6) | copy-start | bytes 9220
  7.2 50.8 %all-gather.6.cloned.1.call-start = ((), (), s32[]{:S(2)}) async-start(), calls=%async_computation.2 | async-start | bytes 2621440 | tf_op jit(solution)/shard_map/all_gather | solution.py:32
  9.3 128.5 %all-gather.4.cloned.1.call-start = ((), (), s32[]{:S(2)}) async-start(), calls=%async_computation.1 | async-start | bytes 9175040 | tf_op jit(solution)/shard_map/all_gather | solution.py:34
  13.2 213.8 %all-gather.8.cloned.1.call-start = ((), (), s32[]{:S(2)}) async-start(), calls=%async_computation.3 | async-start | bytes 10485760 | tf_op jit(solution)/shard_map/all_gather | solution.py:35
  58.0 235.6 %reduce-scatter.2.cloned.1.call-start = ((), (), s32[]{:S(2)}) async-start(), calls=%async_computation.4 | async-start | bytes 28311552 | tf_op jit(solution)/shard_map/reduce_scatter | solution.py:49
Sparse Core Ops, SparseCore 0:
  9.6 48.3 all-gather.5
  60.4 77.4 all-gather.3
  139.7 87.3 all-gather.7
  267.0 26.5 reduce-scatter.1
where the time goes:
time: 307 us; the launch traced here: 305 us
  waiting for transfers between devices  161 us (52%)
  local copies, waits for them, and re-layouts  101 us (33%)
  matrix products  23.4 us (8%)
  between operations  13.9 us (5%)
  other arithmetic  6.12 us (2%)
    all_gather x1, waiting for transfers between devices, on_device(): hidden_piece = lax.all_gather(hidden, 'blk', axis=0, tiled=True)  78.1 us
    gather x2, local copies, waits for them, and re-layouts, on_device(): jnp.take(hidden_blocks, block_rows, axis=1)  67.6 us
    all_gather x1, waiting for transfers between devices, on_device(): grad_full = lax.all_gather(out_grad, 'team', axis=1, tiled=True)  44.7 us
    reduce_scatter x1, waiting for transfers between devices, on_device(): lax.psum_scatter(partial_value, 'dp', scatter_dimension=0, tiled=True)  26.7 us
    dot_general x1, matrix products, on_device(): jnp.einsum('ncki,ncj->ckij', picked_hidden, picked_grad, preferred_elemen...  23.4 us
    reshape x1, local copies, waits for them, and re-layouts, on_device(): grad_piece.reshape(count_rows, column_blocks, BS)  11.9 us
    all_gather x1, waiting for transfers between devices, on_device(): grad_piece = lax.all_gather(grad_full, 'blk', axis=0, tiled=True)  11.2 us
    reshape x1, local copies, waits for them, and re-layouts, on_device(): hidden_blocks = hidden_piece.reshape(count_rows, -1, BS)  10.4 us
  transfers between devices with their start and end apart: 4, of which 4 were waited for; matrix products, arithmetic and copies ran while one was open for 27% of the time, Pallas kernels for 0%

commit v1 on v0

--- a/solution.py
+++ b/solution.py
@@ -29,7 +29,13 @@
     owned_mine = lax.dynamic_index_in_dim(owned_all, owner_index, 0, keepdims=False)
     alive_mine = lax.dynamic_index_in_dim(alive_all, owner_index, 0, keepdims=False)
     block_rows = jnp.take(act_rows[0], owned_mine, axis=0).reshape(-1)
-    grad_full = lax.all_gather(out_grad, "team", axis=1, tiled=True)
+    peers = lax.axis_size("team")
+    moving, blocks = (out_grad, [out_grad])
+    for _ in range(peers - 1):
+        moving = lax.ppermute(moving, "team", [(i, (i + 1) % peers) for i in range(peers)])
+        blocks.insert(0, moving)
+    line = jnp.concatenate(blocks, axis=1)
+    grad_full = jnp.roll(line, (lax.axis_index("team") + 1) * out_grad.shape[1], axis=1)
     grad_mask = alive_mine.astype(jnp.bfloat16)[None, :, None]
     hidden_piece = lax.all_gather(hidden, "blk", axis=0, tiled=True)
     grad_piece = lax.all_gather(grad_full, "blk", axis=0, tiled=True)

time: 307 us -> 262 us (0.85)
  waiting for transfers between devices: 161 us -> 112 us
    all_gather x1, waiting for transfers between devices: 78.1 us -> 31.4 us  [on_device(): hidden_piece = lax.all_gather(hidden, 'blk', axis=0, tiled=True)]
    all_gather x1 -> x0, waiting for transfers between devices: 44.7 us -> none  [on_device(): grad_full = lax.all_gather(out_grad, 'team', axis=1, tiled=True)]
    ppermute x0 -> x3, waiting for transfers between devices: none -> 42.9 us  [on_device(): lax.ppermute(moving, 'team', [(i, (i + 1) % peers) for i in range(peers)])]
    ppermute x0 -> x3, starting transfers between devices: none -> 3.11 us  [on_device(): lax.ppermute(moving, 'team', [(i, (i + 1) % peers) for i in range(peers)])]
  transfers between devices with their start and end apart: 4 -> 6, of which waited for: 4 -> 6; matrix products, arithmetic and copies ran while one was open for 27% -> 31% of each run, Pallas kernels for 0% -> 0%
where the time goes in v1:
time: 262 us; the launch traced here: 260 us
  waiting for transfers between devices  112 us (43%)
  local copies, waits for them, and re-layouts  101 us (39%)
  matrix products  23.4 us (9%)
  between operations  13.9 us (5%)
  other arithmetic  6.12 us (2%)
  starting transfers between devices  3.23 us (1%)
    gather x2, local copies, waits for them, and re-layouts, on_device(): jnp.take(hidden_blocks, block_rows, axis=1)  67.6 us
    ppermute x3, waiting for transfers between devices, on_device(): lax.ppermute(moving, 'team', [(i, (i + 1) % peers) for i in range(peers)])  42.9 us
    all_gather x1, waiting for transfers between devices, on_device(): hidden_piece = lax.all_gather(hidden, 'blk', axis=0, tiled=True)  31.4 us
    reduce_scatter x1, waiting for transfers between devices, on_device(): lax.psum_scatter(partial_value, 'dp', scatter_dimension=0, tiled=True)  26.7 us
    dot_general x1, matrix products, on_device(): jnp.einsum('ncki,ncj->ckij', picked_hidden, picked_grad, preferred_elemen...  23.4 us
    reshape x1, local copies, waits for them, and re-layouts, on_device(): grad_piece.reshape(count_rows, column_blocks, BS)  11.9 us
    all_gather x1, waiting for transfers between devices, on_device(): grad_piece = lax.all_gather(grad_full, 'blk', axis=0, tiled=True)  11.2 us
    reshape x1, local copies, waits for them, and re-layouts, on_device(): hidden_blocks = hidden_piece.reshape(count_rows, -1, BS)  10.4 us
  transfers between devices with their start and end apart: 6, of which 6 were waited for; matrix products, arithmetic and copies ran while one was open for 31% of the time, Pallas kernels for 0%

profile of v1, /device:TPU:0, one launch (start us, length us, event | category | flops | bytes accessed | tf_op | source)
XLA Modules:
  0.0 260.3 jit_solution(9478248536741988886)
XLA Ops:
  7.2 3.9 %copy.19 = bf16[128,7168]{0,1:T(8,128)(2,1)} copy(bf16[128,7168]{1,0:T(8,128)(2,1)} %param.4) | data formatting | bytes 3670016 | tf_op args[0]
  11.2 0.3 copy.22
  11.5 3.1 %collective-permute-start = (bf16[128,2048]{0,1:T(8,128)(2,1)S(1)}, bf16[128,2048]{0,1:T(8,128)(2,1)S(1)}, u32[]{:S(2)}, u32[]{:S(2)}) collective-permute-start(bf16[128,2048]{0,1:T(8,128)(2,1)S(1)} %copy.22), channel_id=1, source_target_pairs={{0,2},{2,4},{4,6},{6,0},{1,3},{3,5},{5,7},{7,1},{8,10},{10,12},{12... | collective-permute-start | bytes 1572872 | tf_op jit(solution)/shard_map/ppermute | solution.py:35
  14.6 13.9 %collective-permute-done = bf16[128,2048]{0,1:T(8,128)(2,1)S(1)} collective-permute-done((bf16[128,2048]{0,1:T(8,128)(2,1)S(1)}, bf16[128,2048]{0,1:T(8,128)(2,1)S(1)}, u32[]{:S(2)}, u32[]{:S(2)}) %collective-permute-start) | collective-permute-done | bytes 524320 | tf_op jit(solution)/shard_map/ppermute | solution.py:35
  28.6 14.9 %collective-permute-done.1 = bf16[128,2048]{0,1:T(8,128)(2,1)S(1)} collective-permute-done((bf16[128,2048]{0,1:T(8,128)(2,1)S(1)}, bf16[128,2048]{0,1:T(8,128)(2,1)S(1)}, u32[]{:S(2)}, u32[]{:S(2)}) %collective-permute-start.1) | collective-permute-done | bytes 524320 | tf_op jit(solution)/shard_map/ppermute | solution.py:35
  43.4 14.0 %collective-permute-done.2 = bf16[128,2048]{0,1:T(8,128)(2,1)S(1)} collective-permute-done((bf16[128,2048]{0,1:T(8,128)(2,1)S(1)}, bf16[128,2048]{0,1:T(8,128)(2,1)S(1)}, u32[]{:S(2)}, u32[]{:S(2)}) %collective-permute-start.2) | collective-permute-done | bytes 524320 | tf_op jit(solution)/shard_map/ppermute | solution.py:35
  58.1 1.5 constant_dynamic-slice_fusion
  59.6 0.1 copy.18
  59.8 0.1 reduce_window_sum.11
  59.9 0.2 select_reduce_fusion
  60.1 0.1 fusion.10
  60.3 0.6 gather_fusion
  61.1 0.2 and_reduce_fusion
  61.3 31.4 %all-gather.3.cloned.1.call-done = bf16[512,7168]{0,1:T(8,128)(2,1)} async-done(((bf16[128,7168]{0,1:T(8,128)(2,1)}), bf16[512,7168]{0,1:T(8,128)(2,1)}) %all-gather.3.cloned.1.call-update) | async-done | bytes 7340048 | tf_op jit(solution)/shard_map/all_gather | solution.py:40
  92.7 10.4 %copy.20 = bf16[512,56,128]{2,0,1:T(8,128)(2,1)} copy(bf16[512,56,128]{0,2,1:T(8,128)(2,1)} %bitcast.28) | data formatting | bytes 14680064 | tf_op jit(solution)/shard_map/reshape | solution.py:47
  103.1 18.8 %gather_fusion.1 = bf16[288,512,128]{2,1,0:T(8,128)(2,1)} fusion(bf16[512,56,128]{2,0,1:T(8,128)(2,1)} %copy.20, s32[1024]{0:T(1024)S(1)} %pad_clamp_fusion), kind=kCustom, calls=%fused_computation.1 | custom fusion | bytes 75498624 | tf_op jit(solution)/shard_map/jit(_take)/gather | solution.py:48
  121.9 48.8 %copy.21 = bf16[512,24,12,128]{0,3,2,1:T(8,128)(2,1)} copy(bf16[512,24,12,128]{3,0,2,1:T(8,128)(2,1)} %bitcast.24) | data formatting | bytes 75497472 | tf_op jit(solution)/shard_map/jit(_take)/gather | solution.py:48
  170.6 11.2 %all-gather.5.cloned.1.call-done = bf16[512,8192]{0,1:T(8,128)(2,1)} async-done(((bf16[128,8192]{0,1:T(8,128)(2,1)}), bf16[512,8192]{0,1:T(8,128)(2,1)}) %all-gather.5.cloned.1.call-update) | async-done | bytes 8388624 | tf_op jit(solution)/shard_map/all_gather | solution.py:41
  181.9 11.9 %copy.25 = bf16[512,64,128]{2,0,1:T(8,128)(2,1)} copy(bf16[512,64,128]{0,2,1:T(8,128)(2,1)} %bitcast.27) | data formatting | bytes 16777216 | tf_op jit(solution)/shard_map/reshape | solution.py:44
  193.8 4.5 %gather_fusion.2 = bf16[24,512,128]{2,1,0:T(8,128)(2,1)S(1)} fusion(bf16[512,64,128]{2,0,1:T(8,128)(2,1)} %copy.25, s32[1024]{0:T(1024)S(1)} %pad_clamp_fusion.1), kind=kCustom, calls=%fused_computation.2 | custom fusion | bytes 6291552 | tf_op jit(solution)/shard_map/jit(_take)/gather | solution.py:44
  198.3 23.4 %fusion = f32[24,12,128,128]{3,2,1,0:T(8,128)} fusion(bf16[512,24,12,128]{0,3,2,1:T(8,128)(2,1)} %copy.21, pred[24,12]{1,0:T(8,128)(4,1)S(1)} %get-tuple-element.2, bf16[24,512,128]{2,1,0:T(8,128)(2,1)S(1)} %gather_fusion.2, pred[24]{0:T(512)(128)(4,1)S(1)} %compare_and_fusion.1, bf16[24]{0:T(256)(128)(2,1)S(1)} %fusion.13), kind=kOutput, calls=%fused_computation.3 | convolution fusion | flops 4853858304 | bytes 59769192 | tf_op jit(solution)/shard_map/ncki,ncj->ckij/dot_general | solution.py:51
  221.7 26.7 %reduce-scatter.2.cloned.1.call-done = f32[144,128,128]{2,1,0:T(8,128)} async-done(((f32[288,128,128]{2,1,0:T(8,128)}), f32[144,128,128]{2,1,0:T(8,128)}) %reduce-scatter.2.cloned.1.call-update) | async-done | bytes 9437200 | tf_op jit(solution)/shard_map/reduce_scatter | solution.py:55
  248.4 4.7 %multiply_reduce_fusion = f32[144]{0:T(256)S(1)} fusion(f32[144,128,128]{2,1,0:T(8,128)} %reduce-scatter.2.cloned.1.call-done), kind=kLoop, calls=%fused_computation.7 | loop fusion | flops 4718448 | bytes 9437760 | tf_op jit(solution)/shard_map/reduce_sum | solution.py:56
  253.1 0.6 add_sqrt_fusion
  (33 shorter events, 1.0 us)
Async XLA Ops:
  7.2 4.1 %copy-start = (bf16[128,2048]{1,0:T(8,128)(2,1)S(1)}, bf16[128,2048]{1,0:T(8,128)(2,1)}, u32[]{:S(2)}) copy-start(bf16[128,2048]{1,0:T(8,128)(2,1)} %param.5) | copy-start | bytes 1572868
  7.2 85.5 %all-gather.3.cloned.1.call-start = ((), (), s32[]{:S(2)}) async-start(), calls=%async_computation.1 | async-start | bytes 9175040 | tf_op jit(solution)/shard_map/all_gather | solution.py:40
  11.2 170.7 %all-gather.5.cloned.1.call-start = ((), (), s32[]{:S(2)}) async-start(), calls=%async_computation.2 | async-start | bytes 10485760 | tf_op jit(solution)/shard_map/all_gather | solution.py:41
  11.5 17.1 %collective-permute-start = (bf16[128,2048]{0,1:T(8,128)(2,1)S(1)}, bf16[128,2048]{0,1:T(8,128)(2,1)S(1)}, u32[]{:S(2)}, u32[]{:S(2)}) collective-permute-start(bf16[128,2048]{0,1:T(8,128)(2,1)S(1)} %copy.22), channel_id=1, source_target_pairs={{0,2},{2,4},{4,6},{6,0},{1,3},{3,5},{5,7},{7,1},{8,10},{10,12},{12... | collective-permute-start | bytes 1572872 | tf_op jit(solution)/shard_map/ppermute | solution.py:35
  28.6 14.9 %collective-permute-start.1 = (bf16[128,2048]{0,1:T(8,128)(2,1)S(1)}, bf16[128,2048]{0,1:T(8,128)(2,1)S(1)}, u32[]{:S(2)}, u32[]{:S(2)}) collective-permute-start(bf16[128,2048]{0,1:T(8,128)(2,1)S(1)} %collective-permute-done), channel_id=1, source_target_pairs={{0,2},{2,4},{4,6},{6,0},{1,3},{3,5},{5,7},{7,1},{8,10},{10,12},{12... | collective-permute-start | bytes 1572872 | tf_op jit(solution)/shard_map/ppermute | solution.py:35
  43.4 14.0 %collective-permute-start.2 = (bf16[128,2048]{0,1:T(8,128)(2,1)S(1)}, bf16[128,2048]{0,1:T(8,128)(2,1)S(1)}, u32[]{:S(2)}, u32[]{:S(2)}) collective-permute-start(bf16[128,2048]{0,1:T(8,128)(2,1)S(1)} %collective-permute-done.1), channel_id=1, source_target_pairs={{0,2},{2,4},{4,6},{6,0},{1,3},{3,5},{5,7},{7,1},{8,10},{10,12},{12... | collective-permute-start | bytes 1572872 | tf_op jit(solution)/shard_map/ppermute | solution.py:35
  57.9 1.7 copy-start.1
  57.9 1.8 copy-start.2
  59.6 188.8 %reduce-scatter.2.cloned.1.call-start = ((), (), s32[]{:S(2)}) async-start(), calls=%async_computation.3 | async-start | bytes 28311552 | tf_op jit(solution)/shard_map/reduce_scatter | solution.py:55
Sparse Core Ops, SparseCore 0:
  11.3 81.3 all-gather.2
  94.5 87.3 all-gather.4
  221.8 26.5 reduce-scatter.1
